TPU v7x, 32 devices: a whole 2x2x4 slice. The times are simulated.
32 devices in a mesh: space: 8 (over z, x), chan: 4 (over y, core).
Axes of the slice: x: 2, y: 2, z: 4, core: 2. Of those that a mesh axis runs over, the one named last changes fastest.
Arguments:
- features: bfloat16 [256, 8, 1024], P('chan', 'space'), may hold values from -6 to 6
- filters: bfloat16 [27, 256, 256], P(None, 'chan'), may hold values from -0.078125 to 0.078125
- out_bias: float32 [256], P('chan'), may hold values from -1 to 1
- loss_grad: bfloat16 [256, 8, 1024], P('chan', 'space'), may hold values from -6 to 6
Outputs:
- activated: float32 [256, 8, 1024], P('chan', 'space')
- in_grad: float32 [256, 8, 1024], P('chan', 'space')
- filter_grad: float32 [27, 256, 256], P(None, 'chan')
- bias_grad: float32 [256], replicated
All inputs are finite; a program needn't handle non-finite values.
Results may differ from a plain program's by a relative error of at most 0.0031.
Values may be sent and summed in bfloat16 or wider, within the bound.
No kernel may reach another device: no remote copies, remote signals or barrier semaphores. Data moves between devices by JAX's collectives and lax.ppermute only.
A program may use at most 128 MiB of HBM per device.

v0:
```python
import math
import jax
import jax.numpy as jnp
from jax import lax
from jax.sharding import PartitionSpec as P

TAPS = 27
PLANE_H = 32
PLANE_W = 32


def extended(cells, sides, width):
    for axis, dim in sides:
        count = lax.axis_size(axis)
        ends = count - 1
        head = lax.slice_in_dim(cells, 0, width, axis=dim)
        tail = lax.slice_in_dim(cells, cells.shape[dim] - width, cells.shape[dim], axis=dim)
        cells = jnp.concatenate(
            [
                lax.ppermute(tail, axis, [(i, (i + 1) % count) for i in range(ends)]),
                cells,
                lax.ppermute(head, axis, [((i + 1) % count, i) for i in range(ends)]),
            ],
            axis=dim,
        )
    return cells


def plane_pad(volume):
    chans, planes, cells = volume.shape
    grid = volume.reshape(chans, planes, PLANE_H, PLANE_W)
    return jnp.pad(grid, ((0, 0), (0, 0), (1, 1), (1, 1)))


def window(padded, depth_off, row_off, col_off, planes):
    chans = padded.shape[0]
    piece = lax.slice(
        padded,
        (0, depth_off, row_off, col_off),
        (chans, depth_off + planes, row_off + PLANE_H, col_off + PLANE_W),
    )
    return piece.reshape(chans, planes * PLANE_H * PLANE_W)


def contract_lead(left, right):
    return lax.dot_general(
        left, right, (((0,), (0,)), ((), ())), preferred_element_type=jnp.float32
    )


def contract_last(left, right):
    return lax.dot_general(
        left, right, (((1,), (1,)), ((), ())), preferred_element_type=jnp.float32
    )


def depth_rim(volume):
    return extended(volume, (("space", 1),), 1)


def all_channels(volume):
    return lax.all_gather(volume, "chan", axis=0, tiled=True)


def full_view(volume):
    return depth_rim(all_channels(volume))


def body(features, filters, out_bias, loss_grad):
    local_in, planes, cells = features.shape
    local_out = out_bias.shape[0]
    total_out = filters.shape[2]
    voxels = planes * cells
    offsets = [(tap // 9, tap // 3 % 3, tap % 3) for tap in range(TAPS)]
    padded_all = plane_pad(full_view(features))
    columns = lax.all_to_all(filters, "chan", split_axis=2, concat_axis=1, tiled=True)
    summed = jnp.zeros((local_out, voxels), jnp.float32)
    for tap_index, (depth_off, row_off, col_off) in enumerate(offsets):
        piece = window(padded_all, depth_off, row_off, col_off, planes)
        summed = summed + contract_lead(columns[tap_index], piece)
    padded_own = lax.dynamic_slice_in_dim(
        padded_all, lax.axis_index("chan") * local_in, local_in, 0
    )
    pre_act = summed + out_bias[:, None]
    sigmoid = jax.nn.sigmoid(pre_act)
    activated = (pre_act * sigmoid).reshape(local_out, planes, cells)
    grad_pre = (
        loss_grad.reshape(local_out, voxels).astype(jnp.float32)
        * sigmoid
        * (1.0 + pre_act * (1.0 - sigmoid))
    ).astype(jnp.bfloat16)
    grad_full = full_view(grad_pre.reshape(local_out, planes, cells))
    padded_grad = plane_pad(grad_full)
    grad_inner = lax.slice_in_dim(grad_full, 1, 1 + planes, axis=1).reshape(total_out, voxels)
    in_total = jnp.zeros((local_in, voxels), jnp.float32)
    filter_list = []
    for tap_index, (depth_off, row_off, col_off) in enumerate(offsets):
        shifted = window(padded_grad, 2 - depth_off, 2 - row_off, 2 - col_off, planes)
        in_total = in_total + jnp.dot(
            filters[tap_index], shifted, preferred_element_type=jnp.float32
        )
        piece = window(padded_own, depth_off, row_off, col_off, planes)
        filter_list.append(contract_last(piece, grad_inner))
    factor = 1.0 / math.sqrt(voxels * lax.axis_size("space"))
    filter_part = jnp.stack(filter_list, axis=0) * factor
    bias_part = jnp.sum(grad_inner.astype(jnp.float32), axis=1) * factor
    filter_grad, bias_grad = lax.psum((filter_part, bias_part), "space")
    in_grad = in_total.reshape(local_in, planes, cells)
    return (activated, in_grad, filter_grad, bias_grad)


def solution(mesh):
    in_specs = (
        P("chan", "space", None),
        P(None, "chan", None),
        P("chan"),
        P("chan", "space", None),
    )
    out_specs = (P("chan", "space", None), P("chan", "space", None), P(None, "chan", None), P())
    return jax.shard_map(body, mesh=mesh, in_specs=in_specs, out_specs=out_specs, check_vma=False)
```

profile of v0, /device:TPU:0, one launch (start us, length us, event | category | flops | bytes accessed | tf_op | source)
XLA Modules:
  0.0 211.8 jit_solution(13178048618152019697)
XLA Ops:
  7.2 9.0 %all_gather.6 = bf16[256,1,1024]{2,0,1:T(8,128)(2,1)S(1)} all-gather(bf16[64,1,1024]{2,0,1:T(8,128)(2,1)} %param.4), channel_id=1, replica_groups=mesh['space'=8,'chan'=4] {'chan'}, dimensions={0}, use_global_device_ids=true | all-gather | bytes 655360 | tf_op jit(solution)/shard_map/all_gather | solution.py:62
  16.4 1.3 collective-permute-start.1
  17.7 5.3 %collective-permute-start = (bf16[256,1,1024]{0,2,1:T(8,128)(2,1)S(1)}, bf16[256,1,1024]{0,2,1:T(8,128)(2,1)}, u32[]{:S(2)}, u32[]{:S(2)}) collective-permute-start(bf16[256,1,1024]{0,2,1:T(8,128)(2,1)S(1)} %copy.15), channel_id=1, source_target_pairs={{0,4},{4,8},{8,12},{12,16},{16,20},{20,24},{24,28},{1,5},{5,9},{9,... | collective-permute-start | bytes 1572872 | tf_op jit(solution)/shard_map/ppermute | solution.py:20
  23.0 3.0 %copy.18 = bf16[27,64,256]{1,0,2:T(8,128)(2,1)S(1)} copy(bf16[27,64,256]{2,1,0:T(8,128)(2,1)S(1)} %copy-done) | data formatting | bytes 1769472 | tf_op args[1]
  26.1 2.4 %reshape.417 = bf16[4,2,55296]{2,1,0:T(2,128)(2,1)} reshape(bf16[256,27,64]{2,1,0:T(8,128)(2,1)S(1)} %bitcast.575) | data formatting | bytes 1769472
  28.5 3.5 %all-to-all-start = ((bf16[4,2,55296]{2,1,0:T(2,128)(2,1)}), bf16[4,2,55296]{2,1,0:T(2,128)(2,1)S(1)}, u32[]{:S(2)}, u32[]{:S(2)}) async-start(bf16[4,2,55296]{2,1,0:T(2,128)(2,1)} %reshape.417), calls=%async_computation | async-start | bytes 1769472 | tf_op jit(solution)/shard_map/all_to_all | solution.py:76
  32.0 0.5 collective-permute-done.1
  32.6 11.0 %collective-permute-done = bf16[256,1,1024]{0,2,1:T(8,128)(2,1)} collective-permute-done((bf16[256,1,1024]{0,2,1:T(8,128)(2,1)S(1)}, bf16[256,1,1024]{0,2,1:T(8,128)(2,1)}, u32[]{:S(2)}, u32[]{:S(2)}) %collective-permute-start) | collective-permute-done | bytes 524320 | tf_op jit(solution)/shard_map/ppermute | solution.py:20
  43.6 1.4 pad_maximum_fusion
  45.0 3.4 %pad_dynamic-slice_fusion.15 = (bf16[64,1,32,32]{0,3,2,1:T(8,128)(2,1)}, bf16[64,1,32,32]{0,3,2,1:T(8,128)(2,1)}, bf16[64,1,32,32]{0,3,2,1:T(8,128)(2,1)}, bf16[...) fusion(s32[]{:T(128)S(6)} %select_n.3, ...), kind=kLoop, calls=%fused_computation.15 | loop fusion | bytes 3014668 | tf_op jit(solution)/shard_map/slice | solution.py:37
  48.3 4.7 %pad_dynamic-slice_fusion.26 = (bf16[64,1,32,32]{0,3,2,1:T(8,128)(2,1)}, bf16[64,1,32,32]{0,3,2,1:T(8,128)(2,1)}, bf16[64,1,32,32]{0,3,2,1:T(8,128)(2,1)}, bf16[...) fusion(s32[]{:T(128)S(6)} %select_n.3, ...), kind=kLoop, calls=%fused_computation.26 | loop fusion | bytes 3670028 | tf_op jit(solution)/shard_map/slice | solution.py:37
  53.0 2.1 pad_slice_fusion.1
  55.1 4.8 %pad_slice_fusion = (bf16[256,1,32,32]{0,3,2,1:T(8,128)(2,1)}, bf16[256,1,32,32]{0,3,2,1:T(8,128)(2,1)}, bf16[256,1,32,32]{0,3,2,1:T(8,128)(2,1)}, bf16[256,1,32...) fusion(bf16[256,3,32,32]{0,3,2,1:T(8,128)(2,1)S(1)} %bitcast.571), kind=kLoop, calls=%fused_computation.27 | loop fusion | bytes 11534336 | tf_op jit(solution)/shard_map/slice | solution.py:37
  59.9 1.9 reshape.418
  61.8 1.4 copy.24
  63.4 0.6 fusion.108
  64.0 0.7 squeeze.163
  64.8 0.7 squeeze.162
  65.5 0.7 squeeze.164
  66.2 0.7 squeeze.165
  66.9 0.7 squeeze.166
  70.2 1.0 fusion.110
  71.2 1.1 convolution_add_fusion.31
  80.8 0.3 fusion.52
  81.2 7.1 %all-gather = bf16[256,1024]{1,0:T(8,128)(2,1)S(1)} all-gather(bf16[64,1024]{1,0:T(8,128)(2,1)S(1)} %get-tuple-element.124), channel_id=2, replica_groups=mesh['space'=8,'chan'=4] {'chan'}, dimensions={0}, use_global_device_ids=true | all-gather | bytes 655360 | tf_op jit(solution)/shard_map/all_gather | solution.py:62
  88.3 1.3 collective-permute-start.3
  89.6 5.4 %collective-permute-start.2 = (bf16[256,1,1024]{2,0,1:T(8,128)(2,1)S(1)}, bf16[256,1,1024]{2,0,1:T(8,128)(2,1)S(1)}, u32[]{:S(2)}, u32[]{:S(2)}) collective-permute-start(bf16[256,1,1024]{2,0,1:T(8,128)(2,1)S(1)} %bitcast.566), channel_id=1, source_target_pairs={{0,4},{4,8},{8,12},{12,16},{16,20},{20,24},{24,28},{1,5},{5,9},{9,... | collective-permute-start | bytes 1572872 | tf_op jit(solution)/shard_map/ppermute | solution.py:20
  95.0 1.0 copy.21
  95.9 0.3 fusion.50
  96.2 0.3 fusion.49
  96.6 0.3 fusion.48
  96.9 0.3 fusion.47
  97.2 0.3 fusion.46
  97.5 0.3 fusion.45
  97.8 0.3 fusion.44
  98.2 0.3 fusion.43
  98.5 0.3 fusion.42
  98.8 0.3 fusion.41
  99.1 0.3 fusion.40
  99.4 0.3 fusion.39
  99.7 0.3 fusion.38
  100.1 0.3 fusion.37
  100.4 0.3 fusion.36
  100.7 0.3 fusion.35
  101.0 0.3 fusion.34
  101.3 0.3 fusion.33
  101.7 0.3 fusion.32
  102.0 0.3 fusion.31
  102.3 0.3 fusion.30
  102.6 0.3 fusion.29
  102.9 0.3 fusion.28
  103.2 0.3 fusion.27
  103.5 0.3 fusion.26
  103.8 0.3 fusion.25
  104.2 0.3 fusion.24
  104.4 1.4 broadcast_multiply_fusion
  106.0 28.3 %psum.15 = f32[256]{0:T(256)} all-reduce(f32[256]{0:T(256)S(1)} %broadcast_multiply_fusion.1), channel_id=1, replica_groups=mesh['space'=8,'chan'=4] {'space'}, use_global_device_ids=true, to_apply=%region_2.3 | all-reduce | flops 256 | bytes 2048 | tf_op jit(solution)/shard_map/psum | solution.py:107
  134.5 0.7 copy.20
  135.2 0.9 pad_slice_fusion.25
  136.1 3.7 %pad_slice_fusion.24 = (bf16[256,1,32,32]{0,3,2,1:T(8,128)(2,1)S(1)}, bf16[256,1,32,32]{0,3,2,1:T(8,128)(2,1)S(1)}, bf16[256,1,32,32]{0,3,2,1:T(8,128)(2,1)S(1)}...) fusion(bf16[256,3,32,32]{0,3,2,1:T(8,128)(2,1)S(1)} %bitcast.573), kind=kLoop, calls=%fused_computation.51 | loop fusion | bytes 11534336 | tf_op jit(solution)/shard_map/slice | solution.py:37
  140.1 0.3 convolution_add_fusion.15
  147.5 1.0 copy.22
  148.5 53.6 %all-reduce.4.cloned.1.call-done = f32[27,64,256]{2,1,0:T(8,128)} async-done(((f32[27,64,256]{2,1,0:T(8,128)}), f32[27,64,256]{2,1,0:T(8,128)}) %all-reduce.4.cloned.1.call-update) | async-done | bytes 1769488 | tf_op jit(solution)/shard_map/psum | solution.py:107
  202.1 2.9 %copy.52 = f32[27,64,256]{2,1,0:T(8,128)} copy(f32[27,64,256]{2,1,0:T(8,128)} %all-reduce.4.cloned.1.call-done) | data formatting | bytes 3538944
  (202 shorter events, 19.1 us)
Async XLA Ops:
  7.2 15.9 %copy-start = (bf16[27,64,256]{2,1,0:T(8,128)(2,1)S(1)}, bf16[27,64,256]{2,1,0:T(8,128)(2,1)}, u32[]{:S(2)}) copy-start(bf16[27,64,256]{2,1,0:T(8,128)(2,1)} %param.5) | copy-start | bytes 2654212
  16.4 16.2 %collective-permute-start.1 = (bf16[256,1,1024]{0,2,1:T(8,128)(2,1)S(1)}, bf16[256,1,1024]{0,2,1:T(8,128)(2,1)}, u32[]{:S(2)}, u32[]{:S(2)}) collective-permute-start(bf16[256,1,1024]{0,2,1:T(8,128)(2,1)S(1)} %copy.15), channel_id=1, source_target_pairs={{4,0},{8,4},{12,8},{16,12},{20,16},{24,20},{28,24},{5,1},{9,5},{13... | collective-permute-start | bytes 1572872 | tf_op jit(solution)/shard_map/ppermute | solution.py:22
  17.7 25.9 %collective-permute-start = (bf16[256,1,1024]{0,2,1:T(8,128)(2,1)S(1)}, bf16[256,1,1024]{0,2,1:T(8,128)(2,1)}, u32[]{:S(2)}, u32[]{:S(2)}) collective-permute-start(bf16[256,1,1024]{0,2,1:T(8,128)(2,1)S(1)} %copy.15), channel_id=1, source_target_pairs={{0,4},{4,8},{8,12},{12,16},{16,20},{20,24},{24,28},{1,5},{5,9},{9,... | collective-permute-start | bytes 1572872 | tf_op jit(solution)/shard_map/ppermute | solution.py:20
  28.5 31.5 %all-to-all-start = ((bf16[4,2,55296]{2,1,0:T(2,128)(2,1)}), bf16[4,2,55296]{2,1,0:T(2,128)(2,1)S(1)}, u32[]{:S(2)}, u32[]{:S(2)}) async-start(bf16[4,2,55296]{2,1,0:T(2,128)(2,1)} %reshape.417), calls=%async_computation | async-start | bytes 1769472 | tf_op jit(solution)/shard_map/all_to_all | solution.py:76
  32.0 170.1 %all-reduce.4.cloned.1.call-start = ((), (), s32[]{:S(2)}) async-start(), calls=%async_computation.1 | async-start | bytes 3538944 | tf_op jit(solution)/shard_map/psum | solution.py:107
  64.0 6.1 %copy-start.26 = (bf16[256,1,32,32]{0,3,2,1:T(8,128)(2,1)S(1)}, bf16[256,1,32,32]{0,3,2,1:T(8,128)(2,1)}, u32[]{:S(2)}) copy-start(bf16[256,1,32,32]{0,3,2,1:T(8,128)(2,1)} %get-tuple-element.98) | copy-start | bytes 1572868
  64.0 7.2 %copy-start.8 = (bf16[256,1,32,32]{0,3,2,1:T(8,128)(2,1)S(1)}, bf16[256,1,32,32]{0,3,2,1:T(8,128)(2,1)}, u32[]{:S(2)}) copy-start(bf16[256,1,32,32]{0,3,2,1:T(8,128)(2,1)} %get-tuple-element.123) | copy-start | bytes 1572868
  68.3 4.0 %copy-start.25 = (bf16[256,1,32,32]{0,3,2,1:T(8,128)(2,1)S(1)}, bf16[256,1,32,32]{0,3,2,1:T(8,128)(2,1)}, u32[]{:S(2)}) copy-start(bf16[256,1,32,32]{0,3,2,1:T(8,128)(2,1)} %get-tuple-element.99) | copy-start | bytes 1572868
  69.6 3.1 %copy-start.24 = (bf16[256,1,32,32]{0,3,2,1:T(8,128)(2,1)S(1)}, bf16[256,1,32,32]{0,3,2,1:T(8,128)(2,1)}, u32[]{:S(2)}) copy-start(bf16[256,1,32,32]{0,3,2,1:T(8,128)(2,1)} %get-tuple-element.100) | copy-start | bytes 1572868
  69.7 3.0 %copy-start.56 = (bf16[256,64]{0,1:T(8,128)(2,1)S(1)}, bf16[256,64]{0,1:T(8,128)(2,1)}, u32[]{:S(2)}) copy-start(bf16[256,64]{0,1:T(8,128)(2,1)} %squeeze.165) | copy-start | bytes 98308
  69.8 2.5 %copy-start.57 = (bf16[256,64]{0,1:T(8,128)(2,1)S(1)}, bf16[256,64]{0,1:T(8,128)(2,1)}, u32[]{:S(2)}) copy-start(bf16[256,64]{0,1:T(8,128)(2,1)} %squeeze.164) | copy-start | bytes 98308
  71.2 1.8 copy-start.7
  71.2 1.8 copy-start.55
  73.0 1.1 copy-start.21
  73.3 1.2 copy-start.20
  73.7 1.1 copy-start.19
  74.0 1.1 copy-start.18
  74.4 1.1 copy-start.17
  74.7 1.1 copy-start.16
  75.1 1.1 copy-start.6
  75.4 1.1 copy-start.15
  75.8 1.1 copy-start.14
  76.1 1.1 copy-start.13
  76.5 1.1 copy-start.12
  76.9 1.1 copy-start.11
  77.2 1.1 copy-start.10
  77.6 1.1 copy-start.9
  77.9 1.1 copy-start.5
  78.3 1.1 copy-start.4
  78.6 1.1 copy-start.3
  79.0 1.1 copy-start.2
  79.7 1.1 copy-start.54
  79.7 1.1 copy-start.58
  79.7 1.1 copy-start.59
  80.7 15.2 %copy-start.53 = (bf16[64,1,32,32]{0,3,2,1:T(8,128)(2,1)S(1)}, bf16[64,1,32,32]{0,3,2,1:T(8,128)(2,1)}, u32[]{:S(2)}) copy-start(bf16[64,1,32,32]{0,3,2,1:T(8,128)(2,1)} %get-tuple-element.69) | copy-start | bytes 393220
  80.8 15.4 %copy-start.52 = (bf16[64,1,32,32]{0,3,2,1:T(8,128)(2,1)S(1)}, bf16[64,1,32,32]{0,3,2,1:T(8,128)(2,1)}, u32[]{:S(2)}) copy-start(bf16[64,1,32,32]{0,3,2,1:T(8,128)(2,1)} %get-tuple-element.68) | copy-start | bytes 393220
  81.2 15.4 %copy-start.51 = (bf16[64,1,32,32]{0,3,2,1:T(8,128)(2,1)S(1)}, bf16[64,1,32,32]{0,3,2,1:T(8,128)(2,1)}, u32[]{:S(2)}) copy-start(bf16[64,1,32,32]{0,3,2,1:T(8,128)(2,1)} %get-tuple-element.67) | copy-start | bytes 393220
  81.2 15.7 %copy-start.50 = (bf16[64,1,32,32]{0,3,2,1:T(8,128)(2,1)S(1)}, bf16[64,1,32,32]{0,3,2,1:T(8,128)(2,1)}, u32[]{:S(2)}) copy-start(bf16[64,1,32,32]{0,3,2,1:T(8,128)(2,1)} %get-tuple-element.66) | copy-start | bytes 393220
  88.3 46.0 %collective-permute-start.3 = (bf16[256,1,1024]{2,0,1:T(8,128)(2,1)S(1)}, bf16[256,1,1024]{2,0,1:T(8,128)(2,1)S(1)}, u32[]{:S(2)}, u32[]{:S(2)}) collective-permute-start(bf16[256,1,1024]{2,0,1:T(8,128)(2,1)S(1)} %bitcast.565), channel_id=1, source_target_pairs={{4,0},{8,4},{12,8},{16,12},{20,16},{24,20},{28,24},{5,1},{9,5},{13... | collective-permute-start | bytes 1572872 | tf_op jit(solution)/shard_map/ppermute | solution.py:22
  89.6 44.7 %collective-permute-start.2 = (bf16[256,1,1024]{2,0,1:T(8,128)(2,1)S(1)}, bf16[256,1,1024]{2,0,1:T(8,128)(2,1)S(1)}, u32[]{:S(2)}, u32[]{:S(2)}) collective-permute-start(bf16[256,1,1024]{2,0,1:T(8,128)(2,1)S(1)} %bitcast.566), channel_id=1, source_target_pairs={{0,4},{4,8},{8,12},{12,16},{16,20},{20,24},{24,28},{1,5},{5,9},{9,... | collective-permute-start | bytes 1572872 | tf_op jit(solution)/shard_map/ppermute | solution.py:20
  95.9 1.3 copy-start.49
  96.2 1.3 copy-start.48
  96.5 1.3 copy-start.47
  96.9 1.3 copy-start.46
  97.2 1.3 copy-start.45
  97.5 1.3 copy-start.44
  97.8 1.3 copy-start.43
  98.1 1.3 copy-start.42
  98.5 1.3 copy-start.41
  98.8 1.3 copy-start.40
  99.1 1.3 copy-start.39
  99.4 1.3 copy-start.38
  99.7 1.3 copy-start.37
  100.0 1.3 copy-start.36
  100.4 1.3 copy-start.35
  100.7 1.3 copy-start.34
  101.0 1.3 copy-start.33
  101.3 1.3 copy-start.32
  101.6 1.3 copy-start.31
  101.9 1.3 copy-start.30
  102.3 1.3 copy-start.29
  102.6 1.3 copy-start.28
  102.9 1.2 copy-start.27
  136.1 3.7 %copy-start.1 = (bf16[27,64,256]{2,1,0:T(8,128)(2,1)S(1)}, bf16[27,64,256]{2,1,0:T(8,128)(2,1)}, u32[]{:S(2)}) copy-start(bf16[27,64,256]{2,1,0:T(8,128)(2,1)} %param.5) | copy-start | bytes 2654212
  (2 other events, 2.1 us)
Sparse Core Ops, SparseCore 0:
  106.0 96.0 all-reduce.3
where the time goes:
time: 212 us
  waiting for transfers between devices  65.1 us (31%)
  blocking collectives  44.4 us (21%)
  local copies, waits for them, and re-layouts  42.4 us (20%)
  matrix products  25 us (12%)
  starting transfers between devices  16.8 us (8%)
  between operations  14.9 us (7%)
  other arithmetic  3.07 us (1%)
    psum x1, waiting for transfers between devices, body(): filter_grad, bias_grad = lax.psum((filter_part, bias_part), 'space')  53.6 us
    psum x1, blocking collectives, body(): filter_grad, bias_grad = lax.psum((filter_part, bias_part), 'space')  28.3 us
    slice x6, local copies, waits for them, and re-layouts, window(): lax.slice(padded, (0, depth_off, row_off, col_off), (chans, depth_off + p...  19.5 us
    all_gather x2, blocking collectives, all_channels(): return lax.all_gather(volume, 'chan', axis=0, tiled=True)  16.1 us
    unnamed x126, local copies, waits for them, and re-layouts  13.7 us
    ppermute x2, waiting for transfers between devices, extended(): lax.ppermute(tail, axis, [(i, (i + 1) % count) for i in range(ends)])  11 us
    ppermute x2, starting transfers between devices, extended(): lax.ppermute(tail, axis, [(i, (i + 1) % count) for i in range(ends)])  10.7 us
    dot_general x27, matrix products, contract_lead(): lax.dot_general(left, right, (((0,), (0,)), ((), ())), preferred_element_...  9.24 us
  transfers between devices with their start and end apart: 6, of which 3 were waited for; matrix products, arithmetic and copies ran while one was open for 22% of the time, Pallas kernels for 0%

commit v1 on v0

--- a/solution.py
+++ b/solution.py
@@ -7,6 +7,13 @@
 TAPS = 27
 PLANE_H = 32
 PLANE_W = 32
+
+
+def move_the_thing(content):
+    return jnp.concatenate(
+        lax.all_to_all(jnp.stack(jnp.split(content, lax.axis_size("chan"), axis=2)), "chan", 0, 0),
+        axis=1,
+    )
 
 
 def extended(cells, sides, width):
@@ -73,7 +80,7 @@
     voxels = planes * cells
     offsets = [(tap // 9, tap // 3 % 3, tap % 3) for tap in range(TAPS)]
     padded_all = plane_pad(full_view(features))
-    columns = lax.all_to_all(filters, "chan", split_axis=2, concat_axis=1, tiled=True)
+    columns = move_the_thing(filters)
     summed = jnp.zeros((local_out, voxels), jnp.float32)
     for tap_index, (depth_off, row_off, col_off) in enumerate(offsets):
         piece = window(padded_all, depth_off, row_off, col_off, planes)

time: 212 us -> 205 us (0.967)
  local copies, waits for them, and re-layouts: 42.4 us -> 35.2 us
    squeeze x27 -> x0, local copies, waits for them, and re-layouts: 6.08 us -> none  [body(): summed = summed + contract_lead(columns[tap_index], piece)]
    psum x1, waiting for transfers between devices: 53.6 us -> 51.4 us  [body(): filter_grad, bias_grad = lax.psum((filter_part, bias_part), 'space')]
    unnamed x126 -> x115, local copies, waits for them, and re-layouts: 13.7 us -> 12.7 us
  transfers between devices with their start and end apart: 6 -> 6, of which waited for: 3 -> 3; matrix products, arithmetic and copies ran while one was open for 22% -> 23% of each run, Pallas kernels for 0% -> 0%
where the time goes in v1:
time: 205 us
  waiting for transfers between devices  64.6 us (32%)
  blocking collectives  44.5 us (22%)
  local copies, waits for them, and re-layouts  35.2 us (17%)
  matrix products  23.4 us (11%)
  starting transfers between devices  17.4 us (8%)
  between operations  14.9 us (7%)
  other arithmetic  4.86 us (2%)
    psum x1, waiting for transfers between devices, body(): filter_grad, bias_grad = lax.psum((filter_part, bias_part), 'space')  51.4 us
    psum x1, blocking collectives, body(): filter_grad, bias_grad = lax.psum((filter_part, bias_part), 'space')  28.4 us
    slice x6, local copies, waits for them, and re-layouts, window(): lax.slice(padded, (0, depth_off, row_off, col_off), (chans, depth_off + p...  19.1 us
    all_gather x2, blocking collectives, all_channels(): return lax.all_gather(volume, 'chan', axis=0, tiled=True)  16.1 us
    unnamed x115, local copies, waits for them, and re-layouts  12.7 us
    ppermute x2, waiting for transfers between devices, extended(): lax.ppermute(tail, axis, [(i, (i + 1) % count) for i in range(ends)])  11.1 us
    ppermute x2, starting transfers between devices, extended(): lax.ppermute(tail, axis, [(i, (i + 1) % count) for i in range(ends)])  10.6 us
    dot_general x27, matrix products, contract_last(): lax.dot_general(left, right, (((1,), (1,)), ((), ())), preferred_element_...  8.02 us
  transfers between devices with their start and end apart: 6, of which 3 were waited for; matrix products, arithmetic and copies ran while one was open for 23% of the time, Pallas kernels for 0%

profile of v1, /device:TPU:0, one launch (start us, length us, event | category | flops | bytes accessed | tf_op | source)
XLA Modules:
  0.0 204.8 jit_solution(13724851527920847361)
XLA Ops:
  7.2 9.0 %all_gather.6 = bf16[256,1,1024]{2,0,1:T(8,128)(2,1)S(1)} all-gather(bf16[64,1,1024]{2,0,1:T(8,128)(2,1)} %param.4), channel_id=1, replica_groups=mesh['space'=8,'chan'=4] {'chan'}, dimensions={0}, use_global_device_ids=true | all-gather | bytes 655360 | tf_op jit(solution)/shard_map/all_gather | solution.py:69
  16.2 1.0 copy.14
  17.2 1.3 collective-permute-start.1
  18.5 5.3 %collective-permute-start = (bf16[256,1,1024]{0,2,1:T(8,128)(2,1)}, bf16[256,1,1024]{0,2,1:T(8,128)(2,1)}, u32[]{:S(2)}, u32[]{:S(2)}) collective-permute-start(bf16[256,1,1024]{0,2,1:T(8,128)(2,1)} %copy.14), channel_id=1, source_target_pairs={{0,4},{4,8},{8,12},{12,16},{16,20},{20,24},{24,28},{1,5},{5,9},{9,... | collective-permute-start | bytes 1572872 | tf_op jit(solution)/shard_map/ppermute | solution.py:27
  23.8 0.4 slice_bitcast_fusion.3
  24.3 0.5 pad_maximum_fusion
  24.7 2.5 %reshape.422 = bf16[4,2,55296]{2,1,0:T(2,128)(2,1)} reshape(bf16[4,27,64,64]{3,2,1,0:T(8,128)(2,1)S(1)} %pad_maximum_fusion) | data formatting | bytes 1769472
  27.2 4.2 %all-to-all-start = ((bf16[4,2,55296]{2,1,0:T(2,128)(2,1)}), bf16[4,2,55296]{2,1,0:T(2,128)(2,1)}, u32[]{:S(2)}, u32[]{:S(2)}) async-start(bf16[4,2,55296]{2,1,0:T(2,128)(2,1)} %reshape.422), calls=%async_computation | async-start | bytes 1769472 | tf_op jit(solution)/shard_map/all_to_all | solution.py:14
  31.5 2.0 collective-permute-done.1
  33.6 11.1 %collective-permute-done = bf16[256,1,1024]{0,2,1:T(8,128)(2,1)} collective-permute-done((bf16[256,1,1024]{0,2,1:T(8,128)(2,1)}, bf16[256,1,1024]{0,2,1:T(8,128)(2,1)}, u32[]{:S(2)}, u32[]{:S(2)}) %collective-permute-start) | collective-permute-done | bytes 524320 | tf_op jit(solution)/shard_map/ppermute | solution.py:27
  44.7 1.5 pad_maximum_fusion.1
  46.2 3.4 %pad_dynamic-slice_fusion.15 = (bf16[64,1,32,32]{0,3,2,1:T(8,128)(2,1)}, bf16[64,1,32,32]{0,3,2,1:T(8,128)(2,1)}, bf16[64,1,32,32]{0,3,2,1:T(8,128)(2,1)}, bf16[...) fusion(s32[]{:T(128)S(6)} %select_n.3, ...), kind=kLoop, calls=%fused_computation.15 | loop fusion | bytes 3014668 | tf_op jit(solution)/shard_map/slice | solution.py:44
  49.6 4.5 %pad_dynamic-slice_fusion.26 = (bf16[64,1,32,32]{0,3,2,1:T(8,128)(2,1)S(1)}, bf16[64,1,32,32]{0,3,2,1:T(8,128)(2,1)}, bf16[64,1,32,32]{0,3,2,1:T(8,128)(2,1)}, b...) fusion(s32[]{:T(128)S(6)} %select_n.3, ...), kind=kLoop, calls=%fused_computation.26 | loop fusion | bytes 3670028 | tf_op jit(solution)/shard_map/slice | solution.py:44
  54.2 2.1 %pad_slice_fusion.1 = (bf16[256,1,32,32]{0,3,2,1:T(8,128)(2,1)S(1)}, bf16[256,1,32,32]{0,3,2,1:T(8,128)(2,1)}, bf16[256,1,32,32]{0,3,2,1:T(8,128)(2,1)}, bf16[25...) fusion(bf16[256,3,32,32]{0,3,2,1:T(8,128)(2,1)S(1)} %bitcast.500), kind=kLoop, calls=%fused_computation.28 | loop fusion | bytes 7340032 | tf_op jit(solution)/shard_map/slice | solution.py:44
  56.2 4.6 %pad_slice_fusion = (bf16[256,1,32,32]{0,3,2,1:T(8,128)(2,1)}, bf16[256,1,32,32]{0,3,2,1:T(8,128)(2,1)}, bf16[256,1,32,32]{0,3,2,1:T(8,128)(2,1)}, bf16[256,1,32...) fusion(bf16[256,3,32,32]{0,3,2,1:T(8,128)(2,1)S(1)} %bitcast.501), kind=kLoop, calls=%fused_computation.27 | loop fusion | bytes 11534336 | tf_op jit(solution)/shard_map/slice | solution.py:44
  60.9 2.9 %reshape.423 = bf16[4,27,64,64]{3,2,1,0:T(8,128)(2,1)S(1)} reshape(bf16[4,2,55296]{2,1,0:T(2,128)(2,1)} %all-to-all-done) | data formatting | bytes 1769472
  64.0 0.8 copy-done.25
  74.0 0.3 fusion.41
  74.3 7.1 %all-gather = bf16[256,1024]{1,0:T(8,128)(2,1)S(1)} all-gather(bf16[64,1024]{1,0:T(8,128)(2,1)S(1)} %get-tuple-element.128), channel_id=2, replica_groups=mesh['space'=8,'chan'=4] {'chan'}, dimensions={0}, use_global_device_ids=true | all-gather | bytes 655360 | tf_op jit(solution)/shard_map/all_gather | solution.py:69
  81.4 1.3 collective-permute-start.3
  82.7 5.2 %collective-permute-start.2 = (bf16[256,1,1024]{2,0,1:T(8,128)(2,1)S(1)}, bf16[256,1,1024]{2,0,1:T(8,128)(2,1)S(1)}, u32[]{:S(2)}, u32[]{:S(2)}) collective-permute-start(bf16[256,1,1024]{2,0,1:T(8,128)(2,1)S(1)} %bitcast.496), channel_id=1, source_target_pairs={{0,4},{4,8},{8,12},{12,16},{16,20},{20,24},{24,28},{1,5},{5,9},{9,... | collective-permute-start | bytes 1572872 | tf_op jit(solution)/shard_map/ppermute | solution.py:27
  87.9 1.0 copy.18
  88.9 0.3 fusion.39
  89.2 0.3 fusion.38
  89.6 0.3 fusion.37
  89.9 0.3 fusion.36
  90.2 0.3 fusion.35
  90.5 0.3 fusion.34
  90.8 0.3 fusion.33
  91.1 0.3 fusion.32
  91.5 0.3 fusion.31
  91.8 0.3 fusion.30
  92.1 0.3 fusion.29
  92.4 0.3 fusion.28
  92.7 0.3 fusion.27
  93.1 0.3 fusion.26
  93.4 0.3 fusion.25
  93.7 0.3 fusion.24
  94.0 0.3 fusion.23
  94.3 0.3 fusion.22
  94.6 0.3 fusion.21
  95.0 0.3 fusion.20
  95.3 0.3 fusion.19
  95.6 0.3 fusion.18
  95.9 0.3 fusion.17
  96.2 0.3 fusion.16
  96.5 0.3 fusion.15
  96.8 0.3 fusion.14
  97.4 1.4 broadcast_multiply_fusion
  99.0 28.4 %psum.15 = f32[256]{0:T(256)} all-reduce(f32[256]{0:T(256)S(1)} %broadcast_multiply_fusion.1), channel_id=1, replica_groups=mesh['space'=8,'chan'=4] {'space'}, use_global_device_ids=true, to_apply=%region_2.3 | all-reduce | flops 256 | bytes 2048 | tf_op jit(solution)/shard_map/psum | solution.py:114
  127.4 1.3 pad_maximum_fusion.2
  128.7 1.7 copy.17
  130.4 0.9 pad_slice_fusion.25
  131.3 3.7 %pad_slice_fusion.24 = (bf16[256,1,32,32]{0,3,2,1:T(8,128)(2,1)S(1)}, bf16[256,1,32,32]{0,3,2,1:T(8,128)(2,1)S(1)}, bf16[256,1,32,32]{0,3,2,1:T(8,128)(2,1)S(1)}...) fusion(bf16[256,3,32,32]{0,3,2,1:T(8,128)(2,1)S(1)} %bitcast.503), kind=kLoop, calls=%fused_computation.51 | loop fusion | bytes 11534336 | tf_op jit(solution)/shard_map/slice | solution.py:44
  135.3 0.3 convolution_add_fusion.15
  136.1 0.3 convolution_add_fusion.12
  136.4 0.3 convolution_add_fusion.11
  137.6 0.3 convolution_add_fusion.7
  137.9 0.3 convolution_add_fusion.6
  139.0 0.3 convolution_add_fusion.2
  139.3 0.3 convolution_add_fusion.1
  142.7 1.0 copy.19
  143.7 51.4 %all-reduce.4.cloned.1.call-done = f32[27,64,256]{2,1,0:T(8,128)} async-done(((f32[27,64,256]{2,1,0:T(8,128)}), f32[27,64,256]{2,1,0:T(8,128)}) %all-reduce.4.cloned.1.call-update) | async-done | bytes 1769488 | tf_op jit(solution)/shard_map/psum | solution.py:114
  195.1 2.9 %copy.47 = f32[27,64,256]{2,1,0:T(8,128)} copy(f32[27,64,256]{2,1,0:T(8,128)} %all-reduce.4.cloned.1.call-done) | data formatting | bytes 3538944
  (165 shorter events, 15.3 us)
Async XLA Ops:
  7.2 16.7 %copy-start = (bf16[27,64,256]{2,1,0:T(8,128)(2,1)S(1)}, bf16[27,64,256]{2,1,0:T(8,128)(2,1)}, u32[]{:S(2)}) copy-start(bf16[27,64,256]{2,1,0:T(8,128)(2,1)} %param.5) | copy-start | bytes 2654212
  17.2 16.4 %collective-permute-start.1 = (bf16[256,1,1024]{0,2,1:T(8,128)(2,1)}, bf16[256,1,1024]{0,2,1:T(8,128)(2,1)}, u32[]{:S(2)}, u32[]{:S(2)}) collective-permute-start(bf16[256,1,1024]{0,2,1:T(8,128)(2,1)} %copy.14), channel_id=1, source_target_pairs={{4,0},{8,4},{12,8},{16,12},{20,16},{24,20},{28,24},{5,1},{9,5},{13... | collective-permute-start | bytes 1572872 | tf_op jit(solution)/shard_map/ppermute | solution.py:29
  18.5 26.2 %collective-permute-start = (bf16[256,1,1024]{0,2,1:T(8,128)(2,1)}, bf16[256,1,1024]{0,2,1:T(8,128)(2,1)}, u32[]{:S(2)}, u32[]{:S(2)}) collective-permute-start(bf16[256,1,1024]{0,2,1:T(8,128)(2,1)} %copy.14), channel_id=1, source_target_pairs={{0,4},{4,8},{8,12},{12,16},{16,20},{20,24},{24,28},{1,5},{5,9},{9,... | collective-permute-start | bytes 1572872 | tf_op jit(solution)/shard_map/ppermute | solution.py:27
  27.2 33.6 %all-to-all-start = ((bf16[4,2,55296]{2,1,0:T(2,128)(2,1)}), bf16[4,2,55296]{2,1,0:T(2,128)(2,1)}, u32[]{:S(2)}, u32[]{:S(2)}) async-start(bf16[4,2,55296]{2,1,0:T(2,128)(2,1)} %reshape.422), calls=%async_computation | async-start | bytes 1769472 | tf_op jit(solution)/shard_map/all_to_all | solution.py:14
  31.5 163.6 %all-reduce.4.cloned.1.call-start = ((), (), s32[]{:S(2)}) async-start(), calls=%async_computation.1 | async-start | bytes 3538944 | tf_op jit(solution)/shard_map/psum | solution.py:114
  63.8 1.0 copy-start.25
  63.8 1.3 copy-start.7
  63.8 1.6 copy-start.24
  64.0 1.7 copy-start.23
  65.1 1.1 copy-start.6
  65.4 1.1 copy-start.22
  65.7 1.1 copy-start.21
  66.0 1.2 copy-start.20
  66.5 1.1 copy-start.19
  66.8 1.1 copy-start.18
  67.1 1.1 copy-start.17
  67.5 1.2 copy-start.16
  67.9 1.1 copy-start.15
  68.2 1.1 copy-start.5
  68.5 1.1 copy-start.14
  68.9 1.2 copy-start.13
  69.3 1.1 copy-start.12
  69.6 1.1 copy-start.11
  70.0 1.1 copy-start.10
  70.3 1.1 copy-start.9
  70.7 1.1 copy-start.8
  71.0 1.1 copy-start.4
  71.4 1.1 copy-start.3
  71.8 1.1 copy-start.2
  72.1 1.1 copy-start.1
  72.8 1.1 copy-start.52
  72.8 1.1 copy-start.53
  72.8 1.1 copy-start.54
  73.8 15.1 %copy-start.51 = (bf16[64,1,32,32]{0,3,2,1:T(8,128)(2,1)S(1)}, bf16[64,1,32,32]{0,3,2,1:T(8,128)(2,1)}, u32[]{:S(2)}) copy-start(bf16[64,1,32,32]{0,3,2,1:T(8,128)(2,1)} %get-tuple-element.69) | copy-start | bytes 393220
  73.9 15.3 %copy-start.50 = (bf16[64,1,32,32]{0,3,2,1:T(8,128)(2,1)S(1)}, bf16[64,1,32,32]{0,3,2,1:T(8,128)(2,1)}, u32[]{:S(2)}) copy-start(bf16[64,1,32,32]{0,3,2,1:T(8,128)(2,1)} %get-tuple-element.68) | copy-start | bytes 393220
  74.3 15.3 %copy-start.49 = (bf16[64,1,32,32]{0,3,2,1:T(8,128)(2,1)S(1)}, bf16[64,1,32,32]{0,3,2,1:T(8,128)(2,1)}, u32[]{:S(2)}) copy-start(bf16[64,1,32,32]{0,3,2,1:T(8,128)(2,1)} %get-tuple-element.67) | copy-start | bytes 393220
  74.3 15.6 %copy-start.48 = (bf16[64,1,32,32]{0,3,2,1:T(8,128)(2,1)S(1)}, bf16[64,1,32,32]{0,3,2,1:T(8,128)(2,1)}, u32[]{:S(2)}) copy-start(bf16[64,1,32,32]{0,3,2,1:T(8,128)(2,1)} %get-tuple-element.66) | copy-start | bytes 393220
  81.4 46.0 %collective-permute-start.3 = (bf16[256,1,1024]{2,0,1:T(8,128)(2,1)S(1)}, bf16[256,1,1024]{2,0,1:T(8,128)(2,1)S(1)}, u32[]{:S(2)}, u32[]{:S(2)}) collective-permute-start(bf16[256,1,1024]{2,0,1:T(8,128)(2,1)S(1)} %bitcast.495), channel_id=1, source_target_pairs={{4,0},{8,4},{12,8},{16,12},{20,16},{24,20},{28,24},{5,1},{9,5},{13... | collective-permute-start | bytes 1572872 | tf_op jit(solution)/shard_map/ppermute | solution.py:29
  82.7 44.7 %collective-permute-start.2 = (bf16[256,1,1024]{2,0,1:T(8,128)(2,1)S(1)}, bf16[256,1,1024]{2,0,1:T(8,128)(2,1)S(1)}, u32[]{:S(2)}, u32[]{:S(2)}) collective-permute-start(bf16[256,1,1024]{2,0,1:T(8,128)(2,1)S(1)} %bitcast.496), channel_id=1, source_target_pairs={{0,4},{4,8},{8,12},{12,16},{16,20},{20,24},{24,28},{1,5},{5,9},{9,... | collective-permute-start | bytes 1572872 | tf_op jit(solution)/shard_map/ppermute | solution.py:27
  88.9 1.3 copy-start.47
  89.2 1.3 copy-start.46
  89.5 1.3 copy-start.45
  89.9 1.3 copy-start.44
  90.2 1.3 copy-start.43
  90.5 1.3 copy-start.42
  90.8 1.3 copy-start.41
  91.1 1.3 copy-start.40
  91.4 1.3 copy-start.39
  91.8 1.3 copy-start.38
  92.1 1.3 copy-start.37
  92.4 1.3 copy-start.36
  92.7 1.3 copy-start.35
  93.0 1.3 copy-start.34
  93.4 1.3 copy-start.33
  93.7 1.3 copy-start.32
  94.0 1.3 copy-start.31
  94.3 1.3 copy-start.30
  94.6 1.3 copy-start.29
  94.9 1.3 copy-start.28
  95.3 1.3 copy-start.27
  95.6 1.2 copy-start.26
Sparse Core Ops, SparseCore 0:
  98.9 96.1 all-reduce.3
